TPU v7x, 32 devices: a whole 2x2x4 slice. The times are simulated.
32 devices in a mesh: clip: 2 (over x), ha: 4 (over z), wa: 4 (over y, core).
Axes of the slice: x: 2, y: 2, z: 4, core: 2. Of those that a mesh axis runs over, the one named last changes fastest.
Arguments:
- latent_cond: bfloat16 [2, 1, 64, 64, 2560], P('clip', None, 'ha', 'wa')
- latent_uncond: bfloat16 [2, 1, 64, 64, 2560], P('clip', None, 'ha', 'wa')
- qkv_weight: bfloat16 [2560, 3840], P(('clip', 'ha', 'wa')), may hold values from -0.125 to 0.125
- cond_pairs: bfloat16 [2, 2, 256, 1280], P('clip', None, ('ha', 'wa')), may hold values from -6 to 6
- guide_mask: int32 [2, 16], P('clip', ('ha', 'wa')), may hold values 0 or 1
- shifts: int32 [2, 2], P('clip'), may hold values from -4 to 4, as said below
- kernel: float32 [3, 3, 1280], replicated, may hold values from -1.2 to 1.2
Outputs:
- refined: bfloat16 [2, 2, 1, 64, 64, 1280], P('clip', None, None, 'ha', 'wa')
Inputs may be any that keep to these rules, and one draw needn't show every extreme that they name: `shifts`: in every draw clip 0 has row shift 4 and column shift -4.
All inputs are finite; a program needn't handle non-finite values. No bound on the sum of `guide_mask` on one device may be relied on, other than what follows from the above.
Results may differ from a plain program's by a relative error of at most 0.011.
Values may be sent and summed in bfloat16 or wider, within the bound.
No kernel may reach another device: no remote copies, remote signals or barrier semaphores. Data moves between devices by JAX's collectives and lax.ppermute only.
A program may use at most 128 MiB of HBM per device.

v0:
```python
import math
import jax
import jax.numpy as jnp
from jax import lax
from jax.sharding import PartitionSpec as P

HEADS = 10
HD = 128
WIN = 8


def extended(block, sides, width):
    for axis, dim in sides:
        count = lax.axis_size(axis)
        forward = [(i, i + 1) for i in range(count - 1)]
        forward.append((count - 1, 0))
        backward = [(target, source) for source, target in forward]
        low = lax.ppermute(
            lax.slice_in_dim(block, block.shape[dim] - width, None, axis=dim), axis, forward
        )
        high = lax.ppermute(lax.slice_in_dim(block, 0, width, axis=dim), axis, backward)
        block = jnp.concatenate([low, block, high], axis=dim)
    return block


def to_windows(grid_field):
    frames, height, width, channels = grid_field.shape
    grid_field = grid_field.reshape(frames, height // WIN, WIN, width // WIN, WIN, channels)
    grid_field = grid_field.transpose(0, 1, 3, 2, 4, 5)
    return grid_field.reshape(-1, WIN * WIN, channels)


def from_windows(blocks, frames, height, width):
    channels = blocks.shape[-1]
    grid_field = blocks.reshape(frames, height // WIN, width // WIN, WIN, WIN, channels)
    return grid_field.transpose(0, 1, 3, 2, 4, 5).reshape(frames, height, width, channels)


def attend(blocks, cond_pair):
    win_count, win_tokens, _ = blocks.shape
    channels = HEADS * HD
    score_scale = 1.0 / math.sqrt(HD)
    queries = blocks[:, :, :channels].reshape(win_count, win_tokens, HEADS, HD)
    key_rows = blocks[:, :, channels : 2 * channels].reshape(win_count, win_tokens, HEADS, HD)
    values = blocks[:, :, 2 * channels :].reshape(win_count, win_tokens, HEADS, HD)
    scores = (
        jnp.einsum("wqhd,wkhd->whqk", queries, key_rows, preferred_element_type=jnp.float32)
        * score_scale
    )
    if cond_pair is None:
        top_score = jnp.max(scores, axis=-1, keepdims=True)
        near_exp = jnp.exp(scores - top_score)
        near_weights = (near_exp / jnp.sum(near_exp, axis=-1, keepdims=True)).astype(jnp.bfloat16)
        attended = jnp.einsum(
            "whqk,wkhd->wqhd", near_weights, values, preferred_element_type=jnp.float32
        )
    else:
        cond_keys = cond_pair[0].reshape(-1, HEADS, HD)
        cond_values = cond_pair[1].reshape(-1, HEADS, HD)
        far_scores = (
            jnp.einsum("wqhd,khd->whqk", queries, cond_keys, preferred_element_type=jnp.float32)
            * score_scale
        )
        top_score = jnp.maximum(
            jnp.max(scores, axis=-1, keepdims=True), jnp.max(far_scores, axis=-1, keepdims=True)
        )
        near_exp = jnp.exp(scores - top_score)
        far_exp = jnp.exp(far_scores - top_score)
        denom = jnp.sum(near_exp, axis=-1, keepdims=True) + jnp.sum(far_exp, axis=-1, keepdims=True)
        near_weights = (near_exp / denom).astype(jnp.bfloat16)
        far_weights = (far_exp / denom).astype(jnp.bfloat16)
        attended = jnp.einsum(
            "whqk,wkhd->wqhd", near_weights, values, preferred_element_type=jnp.float32
        )
        attended = attended + jnp.einsum(
            "whqk,khd->wqhd", far_weights, cond_values, preferred_element_type=jnp.float32
        )
    return attended.reshape(win_count, win_tokens, channels).astype(jnp.bfloat16)


def on_device(latent_cond, latent_uncond, qkv_weight, cond_pairs, guide_mask, shifts, kernel):
    frames, tile_rows, tile_cols, width_d = latent_cond.shape[1:]
    channels = qkv_weight.shape[1] // 3
    cond_flat = latent_cond.reshape(-1, width_d)
    uncond_flat = latent_uncond.reshape(-1, width_d)
    active = guide_mask[0, 0] > 0
    full_weight = lax.all_gather(qkv_weight, ("clip", "ha", "wa"), axis=0, tiled=True)
    cond_next = jnp.dot(cond_flat, full_weight, preferred_element_type=jnp.float32)
    uncond_next = jnp.dot(uncond_flat, full_weight, preferred_element_type=jnp.float32)
    gathered_pairs = lax.all_gather(cond_pairs, ("ha", "wa"), axis=2, tiled=True)
    projected = jnp.stack([cond_next, uncond_next]).astype(jnp.bfloat16)
    projected = projected.reshape(2, frames, tile_rows, tile_cols, 3 * channels)
    rim_width = WIN // 2
    widened = extended(projected, (("ha", 2), ("wa", 3)), rim_width)
    shift_rows = shifts[0, 0]
    shift_cols = shifts[0, 1]
    shifted = lax.dynamic_slice(
        widened,
        (0, 0, rim_width + shift_rows, rim_width + shift_cols, 0),
        (2, frames, tile_rows, tile_cols, 3 * channels),
    )
    cond_attn = from_windows(
        attend(to_windows(shifted[0]), gathered_pairs[0]), frames, tile_rows, tile_cols
    )
    uncond_attn = lax.cond(
        active,
        lambda: from_windows(attend(to_windows(shifted[1]), None), frames, tile_rows, tile_cols),
        lambda: jnp.zeros_like(cond_attn),
    )
    attn_both = jnp.stack([cond_attn, uncond_attn])
    returned = extended(attn_both, (("ha", 2), ("wa", 3)), rim_width + 1)
    padded_block = lax.dynamic_slice(
        returned,
        (0, 0, rim_width - shift_rows, rim_width - shift_cols, 0),
        (2, frames, tile_rows + 2, tile_cols + 2, channels),
    )
    row_index = lax.broadcasted_iota(jnp.int32, (tile_rows + 2, 1), 0)
    col_index = lax.broadcasted_iota(jnp.int32, (1, tile_cols + 2), 1)
    row_place = lax.axis_index("ha")
    col_place = lax.axis_index("wa")
    keep_rows = ((row_index > 0) | (row_place > 0)) & (
        (row_index < tile_rows + 1) | (row_place < lax.axis_size("ha") - 1)
    )
    keep_cols = ((col_index > 0) | (col_place > 0)) & (
        (col_index < tile_cols + 1) | (col_place < lax.axis_size("wa") - 1)
    )
    keep_both = (keep_rows & keep_cols)[None, None, :, :, None]
    padded_block = jnp.where(keep_both, padded_block, jnp.zeros_like(padded_block))
    summed = padded_block[:, :, 1 : tile_rows + 1, 1 : tile_cols + 1, :].astype(jnp.float32)
    for row_tap in range(3):
        for col_tap in range(3):
            window_part = padded_block[
                :, :, row_tap : row_tap + tile_rows, col_tap : col_tap + tile_cols, :
            ]
            summed = summed + kernel[row_tap, col_tap] * window_part.astype(jnp.float32)
    return summed.astype(jnp.bfloat16)[None]


def solution(mesh):
    placed = (
        P("clip", None, "ha", "wa", None),
        P("clip", None, "ha", "wa", None),
        P(("clip", "ha", "wa"), None),
        P("clip", None, ("ha", "wa"), None),
        P("clip", ("ha", "wa")),
        P("clip", None),
        P(),
    )
    return jax.shard_map(
        on_device,
        mesh=mesh,
        in_specs=placed,
        out_specs=P("clip", None, None, "ha", "wa", None),
        check_vma=False,
    )
```

profile of v0, /device:TPU:0, one launch (start us, length us, event | category | flops | bytes accessed | tf_op | source)
XLA Modules:
  0.0 324.2 jit_solution(3135254465915577953)
XLA Ops:
  6.5 0.7 all-gather.3.cloned.1.call-update
  7.3 1.6 copy.94
  8.9 131.6 %all-gather.3.cloned.1.call-done = bf16[2560,3840]{1,0:T(8,128)(2,1)} async-done(((bf16[80,3840]{1,0:T(8,128)(2,1)}), bf16[2560,3840]{1,0:T(8,128)(2,1)}) %all-gather.3.cloned.1.call-update) | async-done | bytes 19660816 | tf_op jit(solution)/shard_map/all_gather | solution.py:87
  140.5 12.0 %fusion.27 = bf16[1,1,16,16,3840]{4,3,2,1,0:T(8,128)(2,1)S(1)} fusion(bf16[2560,3840]{1,0:T(8,128)(2,1)} %all-gather.3.cloned.1.call-done, bf16[1,1,16,16,2560]{4,3,2,1,0:T(8,128)(2,1)S(1)} %copy-done), kind=kOutput, calls=%fused_computation.31 | convolution fusion | flops 5034147840 | bytes 22937600 | tf_op jit(solution)/shard_map/dot_general | solution.py:89
  152.6 0.3 copy-done.10
  152.8 0.3 copy-done.11
  153.1 5.2 %fusion.30 = bf16[1,1,16,16,3840]{4,3,2,1,0:T(8,128)(2,1)S(1)} fusion(bf16[2560,3840]{1,0:T(8,128)(2,1)S(1)} %copy-done.10, bf16[1,1,16,16,2560]{4,3,2,1,0:T(8,128)(2,1)S(1)} %copy-done.11), kind=kOutput, calls=%fused_computation.32 | convolution fusion | flops 5034147840 | bytes 22937600 | tf_op jit(solution)/shard_map/dot_general | solution.py:88
  158.4 0.2 pad_maximum_fusion.6
  158.6 0.4 collective-permute-start
  159.0 3.5 %collective-permute-start.1 = (bf16[2,1,4,16,3840]{4,3,2,1,0:T(8,128)(2,1)S(1)}, bf16[2,1,4,16,3840]{4,3,2,1,0:T(8,128)(2,1)S(1)}, u32[]{:S(2)}, u32[]{:S(2)}) collective-permute-start(bf16[2,1,4,16,3840]{4,3,2,1,0:T(8,128)(2,1)S(1)} %get-tuple-element.25), channel_id=1, source_target_pairs={{4,0},{8,4},{12,8},{0,12},{5,1},{9,5},{13,9},{1,13},{6,2},{10,6},{... | collective-permute-start | bytes 2949128 | tf_op jit(solution)/shard_map/ppermute | solution.py:21
  162.4 27.9 %collective-permute-done = bf16[2,1,4,16,3840]{4,3,2,1,0:T(8,128)(2,1)S(1)} collective-permute-done((bf16[2,1,4,16,3840]{4,3,2,1,0:T(8,128)(2,1)S(1)}, bf16[2,1,4,16,3840]{4,3,2,1,0:T(8,128)(2,1)S(1)}, u32[]{:S(2)}, u32[]{:S(2)}) %collective-permute-start) | collective-permute-done | bytes 983072 | tf_op jit(solution)/shard_map/ppermute | solution.py:18
  190.4 18.6 %collective-permute-done.1 = bf16[2,1,4,16,3840]{4,3,2,1,0:T(8,128)(2,1)S(1)} collective-permute-done((bf16[2,1,4,16,3840]{4,3,2,1,0:T(8,128)(2,1)S(1)}, bf16[2,1,4,16,3840]{4,3,2,1,0:T(8,128)(2,1)S(1)}, u32[]{:S(2)}, u32[]{:S(2)}) %collective-permute-start.1) | collective-permute-done | bytes 983072 | tf_op jit(solution)/shard_map/ppermute | solution.py:21
  208.9 2.6 pad_maximum_fusion.1
  211.5 1.7 collective-permute-start.3
  213.3 0.6 fusion.80
  217.0 5.0 %fusion.79 = (bf16[1,1,256,1280]{3,1,0,2:T(2,128)(2,1)S(1)}, bf16[1,1,256,1280]{3,1,0,2:T(2,128)(2,1)}) fusion(bf16[1,2,256,1280]{3,1,0,2:T(2,128)(2,1)} %all-gather.5.cloned.1.call-done), kind=kLoop, calls=%fused_computation.117 | loop fusion | bytes 2621440 | tf_op jit(solution)/shard_map/slice | solution.py:59
  222.0 3.7 %copy.121 = bf16[1,1,256,1280]{2,3,1,0:T(8,128)(2,1)} copy(bf16[1,1,256,1280]{3,1,0,2:T(2,128)(2,1)} %get-tuple-element.34) | data formatting | bytes 1310720
  225.6 2.0 copy.122
  227.6 17.0 %collective-permute-done.2 = bf16[2,1,24,4,3840]{4,3,2,1,0:T(4,128)(2,1)} collective-permute-done((bf16[2,1,24,4,3840]{4,3,2,1,0:T(4,128)(2,1)}, bf16[2,1,24,4,3840]{4,3,2,1,0:T(4,128)(2,1)}, u32[]{:S(2)}, u32[]{:S(2)}) %collective-permute-start.2) | collective-permute-done | bytes 1474592 | tf_op jit(solution)/shard_map/ppermute | solution.py:18
  244.6 0.8 collective-permute-done.3
  245.4 8.7 %fusion.34 = bf16[2,1,16,16,3840]{4,3,2,1,0:T(8,128)(2,1)S(1)} fusion(s32[]{:T(128)S(6)} %select_n.16, s32[]{:T(128)S(6)} %select_n.17, bf16[2,1,24,4,3840]{4,3,2,1,0:T(4,128)(2,1)} %collective-permute-done.2, bf16[2,1,4,16,3840]{4,3,2,1,0:T(8,128)(2,1)} %copy-done.4, bf16[1,1,16,16,3840]{4,3,2,1,0:T(8,128)(2,1)} %copy-done.2, ...), kind=kLoop, calls=%fused_computation.40 | loop fusion | flops 23592960 | bytes 12779528 | tf_op jit(solution)/shard_map/concatenate | solution.py:22
  254.4 1.6 copy-done.3
  256.1 0.5 fusion.81
  256.6 0.6 copy-done.6
  257.2 0.6 bitcast_reduce_fusion
  257.8 0.3 fusion.61
  258.1 0.9 fusion.54
  259.1 0.4 convolution_bitcast_fusion.1
  259.6 0.6 copy-done.7
  260.2 1.1 fusion.56
  261.3 0.5 copy.107
  261.8 0.4 convert_element_type.86
  262.2 0.3 conditional.1
  262.6 1.8 collective-permute-start.4
  264.4 6.7 %collective-permute-start.5 = (bf16[2,1,5,16,1280]{4,3,2,1,0:T(8,128)(2,1)S(1)}, bf16[2,1,5,16,1280]{4,3,2,1,0:T(8,128)(2,1)S(1)}, u32[]{:S(2)}, u32[]{:S(2)}) collective-permute-start(bf16[2,1,5,16,1280]{4,3,2,1,0:T(8,128)(2,1)S(1)} %get-tuple-element.32), channel_id=1, source_target_pairs={{4,0},{8,4},{12,8},{0,12},{5,1},{9,5},{13,9},{1,13},{6,2},{10,6},{... | collective-permute-start | bytes 1228808 | tf_op jit(solution)/shard_map/ppermute | solution.py:21
  271.0 8.8 %collective-permute-done.4 = bf16[2,1,5,16,1280]{4,3,2,1,0:T(8,128)(2,1)S(1)} collective-permute-done((bf16[2,1,5,16,1280]{4,3,2,1,0:T(8,128)(2,1)S(1)}, bf16[2,1,5,16,1280]{4,3,2,1,0:T(8,128)(2,1)S(1)}, u32[]{:S(2)}, u32[]{:S(2)}) %collective-permute-start.4) | collective-permute-done | bytes 409632 | tf_op jit(solution)/shard_map/ppermute | solution.py:18
  279.8 1.1 collective-permute-done.5
  281.0 0.3 pad_maximum_fusion
  281.2 0.2 fusion.78
  281.5 0.5 copy.109
  282.1 4.6 %collective-permute-start.6 = (bf16[2,1,26,5,1280]{4,0,3,2,1:T(2,128)(2,1)S(1)}, bf16[2,1,26,5,1280]{4,0,3,2,1:T(2,128)(2,1)S(1)}, u32[]{:S(2)}, u32[]{:S(2)}) collective-permute-start(bf16[2,1,26,5,1280]{4,0,3,2,1:T(2,128)(2,1)S(1)} %copy.109), channel_id=1, source_target_pairs={{0,1},{1,2},{2,3},{3,0},{4,5},{5,6},{6,7},{7,4},{8,9},{9,10},{10,1... | collective-permute-start | bytes 1996808 | tf_op jit(solution)/shard_map/ppermute | solution.py:18
  286.7 1.4 copy.110
  288.1 5.9 %collective-permute-start.7 = (bf16[2,1,26,5,1280]{4,0,3,2,1:T(2,128)(2,1)}, bf16[2,1,26,5,1280]{4,0,3,2,1:T(2,128)(2,1)}, u32[]{:S(2)}, u32[]{:S(2)}) collective-permute-start(bf16[2,1,26,5,1280]{4,0,3,2,1:T(2,128)(2,1)} %copy.110), channel_id=1, source_target_pairs={{1,0},{2,1},{3,2},{0,3},{5,4},{6,5},{7,6},{4,7},{9,8},{10,9},{11,1... | collective-permute-start | bytes 1996808 | tf_op jit(solution)/shard_map/ppermute | solution.py:21
  296.6 7.5 %collective-permute-done.6 = bf16[2,1,26,5,1280]{4,0,3,2,1:T(2,128)(2,1)S(1)} collective-permute-done((bf16[2,1,26,5,1280]{4,0,3,2,1:T(2,128)(2,1)S(1)}, bf16[2,1,26,5,1280]{4,0,3,2,1:T(2,128)(2,1)S(1)}, u32[]{:S(2)}, u32[]{:S(2)}) %collective-permute-start.6) | collective-permute-done | bytes 665632 | tf_op jit(solution)/shard_map/ppermute | solution.py:18
  304.2 3.6 %collective-permute-done.7 = bf16[2,1,26,5,1280]{4,0,3,2,1:T(2,128)(2,1)} collective-permute-done((bf16[2,1,26,5,1280]{4,0,3,2,1:T(2,128)(2,1)}, bf16[2,1,26,5,1280]{4,0,3,2,1:T(2,128)(2,1)}, u32[]{:S(2)}, u32[]{:S(2)}) %collective-permute-start.7) | collective-permute-done | bytes 665632 | tf_op jit(solution)/shard_map/ppermute | solution.py:21
  307.7 1.2 copy.112
  308.9 4.3 %fusion.50 = bf16[2,1,18,18,1280]{4,3,2,1,0:T(8,128)(2,1)S(1)} fusion(s32[]{:T(128)S(6)} %select_n.18, s32[]{:T(128)S(6)} %select_n.19, bf16[2,1,26,5,1280]{4,3,2,1,0:T(8,128)(2,1)S(1)} %copy.111, bf16[2,1,5,16,1280]{4,3,2,1,0:T(8,128)(2,1)S(1)} %collective-permute-done.4, bf16[1,1,16,16,1280]{4,3,2,1,0:T(8,128)(2,1)S(1)} %bitcast.131, ...), kind=kLoop, calls=%fused_computation.61 | loop fusion | flops 10782720 | bytes 5120332 | tf_op jit(solution)/shard_map/jit(_where)/select_n | solution.py:128
  313.3 4.0 %fusion.60 = bf16[1,2,1,16,16,1280]{5,4,3,2,1,0:T(8,128)(2,1)} fusion(bf16[2,1,18,18,1280]{4,3,2,1,0:T(8,128)(2,1)S(1)} %fusion.50, f32[1280]{0:T(1024)S(1)} %get-tuple-element.17, f32[1280]{0:T(1024)S(1)} %get-tuple-element.18, f32[1280]{0:T(1024)S(1)} %get-tuple-element.11, f32[1280]{0:T(1024)S(1)} %get-tuple-element.12, f32[1280]{0:T(1024)S(1)} %get-tuple-element.13, ...), kind=kLoop, calls=%fused_computation.81 | loop fusion | flops 18350080 | bytes 13153280 | tf_op jit(solution)/shard_map/broadcast_in_dim | solution.py:136
  (38 shorter events, 1.0 us)
Async XLA Ops:
  6.5 134.0 %copy-start = (bf16[1,1,16,16,2560]{4,3,2,1,0:T(8,128)(2,1)S(1)}, bf16[1,1,16,16,2560]{4,3,2,1,0:T(8,128)(2,1)}, u32[]{:S(2)}) copy-start(bf16[1,1,16,16,2560]{4,3,2,1,0:T(8,128)(2,1)} %param.10) | copy-start | bytes 3932164
  6.5 134.0 %all-gather.3.cloned.1.call-start = ((), (), s32[]{:S(2)}) async-start(), calls=%async_computation | async-start | bytes 20275200 | tf_op jit(solution)/shard_map/all_gather | solution.py:87
  7.3 209.7 %all-gather.5.cloned.1.call-start = ((), (), s32[]{:S(2)}) async-start(), calls=%async_computation.1 | async-start | bytes 1392640 | tf_op jit(solution)/shard_map/all_gather | solution.py:90
  140.5 12.3 %copy-start.10 = (bf16[2560,3840]{1,0:T(8,128)(2,1)S(1)}, bf16[2560,3840]{1,0:T(8,128)(2,1)}, u32[]{:S(2)}) copy-start(bf16[2560,3840]{1,0:T(8,128)(2,1)} %all-gather.3.cloned.1.call-done) | copy-start | bytes 58982404
  140.5 12.6 %copy-start.11 = (bf16[1,1,16,16,2560]{4,3,2,1,0:T(8,128)(2,1)S(1)}, bf16[1,1,16,16,2560]{4,3,2,1,0:T(8,128)(2,1)}, u32[]{:S(2)}) copy-start(bf16[1,1,16,16,2560]{4,3,2,1,0:T(8,128)(2,1)} %param.9) | copy-start | bytes 3932164
  158.4 50.6 %copy-start.2 = (bf16[1,1,16,16,3840]{4,3,2,1,0:T(8,128)(2,1)}, bf16[1,1,16,16,3840]{4,3,2,1,0:T(8,128)(2,1)S(1)}, u32[]{:S(2)}) copy-start(bf16[1,1,16,16,3840]{4,3,2,1,0:T(8,128)(2,1)S(1)} %fusion.30) | copy-start | bytes 5898244
  158.6 31.8 %collective-permute-start = (bf16[2,1,4,16,3840]{4,3,2,1,0:T(8,128)(2,1)S(1)}, bf16[2,1,4,16,3840]{4,3,2,1,0:T(8,128)(2,1)S(1)}, u32[]{:S(2)}, u32[]{:S(2)}) collective-permute-start(bf16[2,1,4,16,3840]{4,3,2,1,0:T(8,128)(2,1)S(1)} %get-tuple-element.24), channel_id=1, source_target_pairs={{0,4},{4,8},{8,12},{12,0},{1,5},{5,9},{9,13},{13,1},{2,6},{6,10},{... | collective-permute-start | bytes 2949128 | tf_op jit(solution)/shard_map/ppermute | solution.py:18
  159.0 54.3 %copy-start.9 = (s32[1,2]{1,0:T(1,128)S(1)}, s32[1,2]{1,0:T(1,128)}, u32[]{:S(2)}) copy-start(s32[1,2]{1,0:T(1,128)} %param.14) | copy-start | bytes 28
  159.0 50.0 %collective-permute-start.1 = (bf16[2,1,4,16,3840]{4,3,2,1,0:T(8,128)(2,1)S(1)}, bf16[2,1,4,16,3840]{4,3,2,1,0:T(8,128)(2,1)S(1)}, u32[]{:S(2)}, u32[]{:S(2)}) collective-permute-start(bf16[2,1,4,16,3840]{4,3,2,1,0:T(8,128)(2,1)S(1)} %get-tuple-element.25), channel_id=1, source_target_pairs={{4,0},{8,4},{12,8},{0,12},{5,1},{9,5},{13,9},{1,13},{6,2},{10,6},{... | collective-permute-start | bytes 2949128 | tf_op jit(solution)/shard_map/ppermute | solution.py:21
  190.4 21.1 %copy-start.4 = (bf16[2,1,4,16,3840]{4,3,2,1,0:T(8,128)(2,1)}, bf16[2,1,4,16,3840]{4,3,2,1,0:T(8,128)(2,1)S(1)}, u32[]{:S(2)}) copy-start(bf16[2,1,4,16,3840]{4,3,2,1,0:T(8,128)(2,1)S(1)} %collective-permute-done) | copy-start | bytes 2949124
  208.9 2.6 copy-start.5
  211.5 33.1 %collective-permute-start.2 = (bf16[2,1,24,4,3840]{4,3,2,1,0:T(4,128)(2,1)}, bf16[2,1,24,4,3840]{4,3,2,1,0:T(4,128)(2,1)}, u32[]{:S(2)}, u32[]{:S(2)}) collective-permute-start(bf16[2,1,24,4,3840]{4,3,2,1,0:T(4,128)(2,1)} %get-tuple-element.23), channel_id=1, source_target_pairs={{0,1},{1,2},{2,3},{3,0},{4,5},{5,6},{6,7},{7,4},{8,9},{9,10},{10,1... | collective-permute-start | bytes 4423688 | tf_op jit(solution)/shard_map/ppermute | solution.py:18
  211.5 33.9 %collective-permute-start.3 = (bf16[2,1,24,4,3840]{4,3,2,1,0:T(4,128)(2,1)}, bf16[2,1,24,4,3840]{4,3,2,1,0:T(4,128)(2,1)}, u32[]{:S(2)}, u32[]{:S(2)}) collective-permute-start(bf16[2,1,24,4,3840]{4,3,2,1,0:T(4,128)(2,1)} %get-tuple-element.22), channel_id=1, source_target_pairs={{1,0},{2,1},{3,2},{0,3},{5,4},{6,5},{7,6},{4,7},{9,8},{10,9},{11,1... | collective-permute-start | bytes 4423688 | tf_op jit(solution)/shard_map/ppermute | solution.py:21
  254.1 1.9 copy-start.3
  256.1 1.1 copy-start.6
  259.1 1.1 copy-start.7
  262.6 17.2 %collective-permute-start.4 = (bf16[2,1,5,16,1280]{4,3,2,1,0:T(8,128)(2,1)S(1)}, bf16[2,1,5,16,1280]{4,3,2,1,0:T(8,128)(2,1)S(1)}, u32[]{:S(2)}, u32[]{:S(2)}) collective-permute-start(bf16[2,1,5,16,1280]{4,3,2,1,0:T(8,128)(2,1)S(1)} %get-tuple-element.31), channel_id=1, source_target_pairs={{0,4},{4,8},{8,12},{12,0},{1,5},{5,9},{9,13},{13,1},{2,6},{6,10},{... | collective-permute-start | bytes 1228808 | tf_op jit(solution)/shard_map/ppermute | solution.py:18
  264.4 16.6 %collective-permute-start.5 = (bf16[2,1,5,16,1280]{4,3,2,1,0:T(8,128)(2,1)S(1)}, bf16[2,1,5,16,1280]{4,3,2,1,0:T(8,128)(2,1)S(1)}, u32[]{:S(2)}, u32[]{:S(2)}) collective-permute-start(bf16[2,1,5,16,1280]{4,3,2,1,0:T(8,128)(2,1)S(1)} %get-tuple-element.32), channel_id=1, source_target_pairs={{4,0},{8,4},{12,8},{0,12},{5,1},{9,5},{13,9},{1,13},{6,2},{10,6},{... | collective-permute-start | bytes 1228808 | tf_op jit(solution)/shard_map/ppermute | solution.py:21
  281.5 14.9 %copy-start.8 = (f32[3,3,1280]{2,1,0:T(4,128)S(1)}, f32[3,3,1280]{2,1,0:T(4,128)}, u32[]{:S(2)}) copy-start(f32[3,3,1280]{2,1,0:T(4,128)} %param.15) | copy-start | bytes 138244
  282.1 22.0 %collective-permute-start.6 = (bf16[2,1,26,5,1280]{4,0,3,2,1:T(2,128)(2,1)S(1)}, bf16[2,1,26,5,1280]{4,0,3,2,1:T(2,128)(2,1)S(1)}, u32[]{:S(2)}, u32[]{:S(2)}) collective-permute-start(bf16[2,1,26,5,1280]{4,0,3,2,1:T(2,128)(2,1)S(1)} %copy.109), channel_id=1, source_target_pairs={{0,1},{1,2},{2,3},{3,0},{4,5},{5,6},{6,7},{7,4},{8,9},{9,10},{10,1... | collective-permute-start | bytes 1996808 | tf_op jit(solution)/shard_map/ppermute | solution.py:18
  288.1 19.7 %collective-permute-start.7 = (bf16[2,1,26,5,1280]{4,0,3,2,1:T(2,128)(2,1)}, bf16[2,1,26,5,1280]{4,0,3,2,1:T(2,128)(2,1)}, u32[]{:S(2)}, u32[]{:S(2)}) collective-permute-start(bf16[2,1,26,5,1280]{4,0,3,2,1:T(2,128)(2,1)} %copy.110), channel_id=1, source_target_pairs={{1,0},{2,1},{3,2},{0,3},{5,4},{6,5},{7,6},{4,7},{9,8},{10,9},{11,1... | collective-permute-start | bytes 1996808 | tf_op jit(solution)/shard_map/ppermute | solution.py:21
  313.3 4.1 %copy-start.1 = (bf16[1,1,16,16,2560]{4,3,2,1,0:T(8,128)(2,1)S(1)}, bf16[1,1,16,16,2560]{4,3,2,1,0:T(8,128)(2,1)}, u32[]{:S(2)}) copy-start(bf16[1,1,16,16,2560]{4,3,2,1,0:T(8,128)(2,1)} %param.10) | copy-start | bytes 3932164
Sparse Core Ops, SparseCore 0:
  10.2 130.2 all-gather.2
  142.8 51.0 all-gather.4
where the time goes:
time: 325 us; the launch traced here: 324 us
  waiting for transfers between devices  218 us (67%)
  starting transfers between devices  24.6 us (8%)
  other arithmetic  21.5 us (7%)
  local copies, waits for them, and re-layouts  21.2 us (7%)
  matrix products  19.9 us (6%)
  between operations  19.2 us (6%)
    all_gather x1, waiting for transfers between devices, on_device(): lax.all_gather(qkv_weight, ('clip', 'ha', 'wa'), axis=0, tiled=True)  132 us
    ppermute x4, waiting for transfers between devices, extended(): lax.ppermute(lax.slice_in_dim(block, block.shape[dim] - width, None, axis...  61.2 us
    ppermute x4, waiting for transfers between devices, extended(): lax.ppermute(lax.slice_in_dim(block, 0, width, axis=dim), axis, backward)  24 us
    ppermute x4, starting transfers between devices, extended(): lax.ppermute(lax.slice_in_dim(block, 0, width, axis=dim), axis, backward)  17.7 us
    dot_general x1, matrix products, on_device(): jnp.dot(uncond_flat, full_weight, preferred_element_type=jnp.float32)  12 us
    concatenate x3, other arithmetic, extended(): block = jnp.concatenate([low, block, high], axis=dim)  11.5 us
    unnamed x28, local copies, waits for them, and re-layouts  10.8 us
    ppermute x4, starting transfers between devices, extended(): lax.ppermute(lax.slice_in_dim(block, block.shape[dim] - width, None, axis...  6.78 us
  transfers between devices with their start and end apart: 10, of which 9 were waited for; matrix products, arithmetic and copies ran while one was open for 11% of the time, Pallas kernels for 0%

commit v1 on v0

--- a/solution.py
+++ b/solution.py
@@ -84,7 +84,24 @@
     cond_flat = latent_cond.reshape(-1, width_d)
     uncond_flat = latent_uncond.reshape(-1, width_d)
     active = guide_mask[0, 0] > 0
-    full_weight = lax.all_gather(qkv_weight, ("clip", "ha", "wa"), axis=0, tiled=True)
+    ways, here, step = (
+        lax.axis_size(("clip", "ha", "wa")),
+        lax.axis_index(("clip", "ha", "wa")),
+        qkv_weight.shape[0],
+    )
+    line, have = (qkv_weight, 1)
+    while have < ways:
+        line = jnp.concatenate(
+            [
+                line,
+                lax.ppermute(
+                    line, ("clip", "ha", "wa"), [(d, (d - have) % ways) for d in range(ways)]
+                ),
+            ],
+            axis=0,
+        )
+        have = 2 * have
+    full_weight = jnp.roll(line, here * step, axis=0)
     cond_next = jnp.dot(cond_flat, full_weight, preferred_element_type=jnp.float32)
     uncond_next = jnp.dot(uncond_flat, full_weight, preferred_element_type=jnp.float32)
     gathered_pairs = lax.all_gather(cond_pairs, ("ha", "wa"), axis=2, tiled=True)

time: 325 us -> 745 us (2.29)
  waiting for transfers between devices: 218 us -> 592 us
  local copies, waits for them, and re-layouts: 21.2 us -> 56.3 us
    ppermute x0 -> x5, waiting for transfers between devices: none -> 507 us  [on_device(): lax.ppermute(line, ('clip', 'ha', 'wa'), [(d, (d - have) % ways) for d in...]
    all_gather x1 -> x0, waiting for transfers between devices: 132 us -> none  [on_device(): lax.all_gather(qkv_weight, ('clip', 'ha', 'wa'), axis=0, tiled=True)]
    unnamed x28 -> x52, local copies, waits for them, and re-layouts: 10.8 us -> 32.9 us
    concatenate x0 -> x2, local copies, waits for them, and re-layouts: none -> 12.9 us  [the longest x1 8.15 us: on_device(): full_weight = jnp.roll(line, here * step, axis=0)]
    ppermute x0 -> x5, starting transfers between devices: none -> 12.1 us  [on_device(): lax.ppermute(line, ('clip', 'ha', 'wa'), [(d, (d - have) % ways) for d in...]
  transfers between devices with their start and end apart: 10 -> 14, of which waited for: 9 -> 13; matrix products, arithmetic and copies ran while one was open for 11% -> 9% of each run, Pallas kernels for 0% -> 0%
where the time goes in v1:
time: 745 us; the launch traced here: 743 us
  waiting for transfers between devices  592 us (79%)
  local copies, waits for them, and re-layouts  56.3 us (8%)
  starting transfers between devices  28.9 us (4%)
  other arithmetic  23.5 us (3%)
  matrix products  22 us (3%)
  between operations  19.6 us (3%)
    ppermute x5, waiting for transfers between devices, on_device(): lax.ppermute(line, ('clip', 'ha', 'wa'), [(d, (d - have) % ways) for d in...  507 us
    ppermute x4, waiting for transfers between devices, extended(): lax.ppermute(lax.slice_in_dim(block, block.shape[dim] - width, None, axis...  56.9 us
    unnamed x52, local copies, waits for them, and re-layouts  32.9 us
    ppermute x4, waiting for transfers between devices, extended(): lax.ppermute(lax.slice_in_dim(block, 0, width, axis=dim), axis, backward)  28.2 us
    ppermute x4, starting transfers between devices, extended(): lax.ppermute(lax.slice_in_dim(block, 0, width, axis=dim), axis, backward)  16.1 us
  transfers between devices with their start and end apart: 14, of which 13 were waited for; matrix products, arithmetic and copies ran while one was open for 9% of the time, Pallas kernels for 0%

profile of v1, /device:TPU:0, one launch (start us, length us, event | category | flops | bytes accessed | tf_op | source)
XLA Modules:
  0.0 742.6 jit_solution(5612002004047145010)
XLA Ops:
  6.5 6.4 collective-permute-start
  12.9 8.0 %collective-permute-done = bf16[80,3840]{1,0:T(8,128)(2,1)S(1)} collective-permute-done((bf16[80,3840]{1,0:T(8,128)(2,1)}, bf16[80,3840]{1,0:T(8,128)(2,1)S(1)}, u32[]{:S(2)}, u32[]{:S(2)}) %collective-permute-start) | collective-permute-done | bytes 614432 | tf_op jit(solution)/shard_map/ppermute | solution.py:97
  20.9 1.4 pad_maximum_fusion.7
  23.0 25.7 %collective-permute-done.1 = bf16[160,3840]{1,0:T(8,128)(2,1)S(1)} collective-permute-done((bf16[160,3840]{1,0:T(8,128)(2,1)S(1)}, bf16[160,3840]{1,0:T(8,128)(2,1)S(1)}, u32[]{:S(2)}, u32[]{:S(2)}) %collective-permute-start.1) | collective-permute-done | bytes 1228832 | tf_op jit(solution)/shard_map/ppermute | solution.py:97
  48.8 0.9 collective-permute-start.2
  49.7 54.6 %collective-permute-done.2 = bf16[320,3840]{1,0:T(8,128)(2,1)S(1)} collective-permute-done((bf16[320,3840]{1,0:T(8,128)(2,1)S(1)}, bf16[320,3840]{1,0:T(8,128)(2,1)S(1)}, u32[]{:S(2)}, u32[]{:S(2)}) %collective-permute-start.2) | collective-permute-done | bytes 2457632 | tf_op jit(solution)/shard_map/ppermute | solution.py:97
  104.7 2.8 collective-permute-start.3
  107.4 0.9 constant_dynamic-update-slice_fusion.4
  108.3 0.9 constant_dynamic-update-slice_fusion.3
  109.2 1.2 constant_dynamic-update-slice_fusion.2
  110.5 1.8 constant_dynamic-update-slice_fusion.1
  112.2 207.3 %collective-permute-done.3 = bf16[640,3840]{1,0:T(8,128)(2,1)S(1)} collective-permute-done((bf16[640,3840]{1,0:T(8,128)(2,1)S(1)}, bf16[640,3840]{1,0:T(8,128)(2,1)S(1)}, u32[]{:S(2)}, u32[]{:S(2)}) %collective-permute-start.3) | collective-permute-done | bytes 4915232 | tf_op jit(solution)/shard_map/ppermute | solution.py:97
  319.5 4.7 constant_dynamic-update-slice_fusion
  324.7 1.5 collective-permute-start.4
  326.9 211.3 %collective-permute-done.4 = bf16[1280,3840]{1,0:T(8,128)(2,1)} collective-permute-done((bf16[1280,3840]{1,0:T(8,128)(2,1)}, bf16[1280,3840]{1,0:T(8,128)(2,1)}, u32[]{:S(2)}, u32[]{:S(2)}) %collective-permute-start.4) | collective-permute-done | bytes 9830432 | tf_op jit(solution)/shard_map/ppermute | solution.py:97
  538.2 8.2 %constant_dynamic-update-slice_fusion.11 = bf16[5120,3840]{1,0:T(8,128)(2,1)} fusion(bf16[5120,3840]{1,0:T(8,128)(2,1)} %get-tuple-element.25, bf16[1280,3840]{1,0:T(8,128)(2,1)} %collective-permute-done.4), kind=kLoop, calls=%fused_computation.111 | loop fusion | bytes 19660800
  546.4 0.9 constant_dynamic-update-slice_fusion.10
  547.3 2.0 constant_dynamic-update-slice_fusion.9
  549.3 1.1 constant_dynamic-update-slice_fusion.8
  550.4 1.6 constant_dynamic-update-slice_fusion.7
  552.0 1.7 copy-done.5
  553.7 2.5 constant_dynamic-update-slice_fusion.6
  556.2 8.1 %constant_dynamic-update-slice_fusion.5 = bf16[5120,3840]{1,0:T(8,128)(2,1)} fusion(bf16[5120,3840]{1,0:T(8,128)(2,1)} %constant_dynamic-update-slice_fusion.6, bf16[1280,3840]{1,0:T(8,128)(2,1)} %collective-permute-done.4), kind=kLoop, calls=%fused_computation.105 | loop fusion | bytes 19660800 | tf_op jit(solution)/shard_map/jit(_roll_dynamic)/concatenate | solution.py:104
  564.3 9.7 %fusion.24 = bf16[3840,256]{0,1:T(8,128)(2,1)S(1)} fusion(bf16[256,2560]{1,0:T(8,128)(2,1)S(1)} %bitcast.115, bf16[5120,3840]{1,0:T(8,128)(2,1)} %constant_dynamic-update-slice_fusion.5, s32[]{:T(128)S(6)} %select_n.30), kind=kOutput, calls=%fused_computation.30 | convolution fusion | flops 5034147840 | bytes 22937604 | tf_op jit(solution)/shard_map/dot_general | solution.py:105
  574.1 9.6 %fusion.21 = bf16[3840,256]{0,1:T(8,128)(2,1)S(1)} fusion(bf16[256,2560]{1,0:T(8,128)(2,1)S(1)} %bitcast.134, bf16[5120,3840]{1,0:T(8,128)(2,1)} %constant_dynamic-update-slice_fusion.5, s32[]{:T(128)S(6)} %select_n.30), kind=kOutput, calls=%fused_computation.29 | convolution fusion | flops 5034147840 | bytes 22937604 | tf_op jit(solution)/shard_map/dot_general | solution.py:106
  584.0 3.8 collective-permute-start.6
  587.8 22.6 %collective-permute-done.5 = bf16[2,1,4,16,3840]{4,3,2,1,0:T(8,128)(2,1)S(1)} collective-permute-done((bf16[2,1,4,16,3840]{4,3,2,1,0:T(8,128)(2,1)S(1)}, bf16[2,1,4,16,3840]{4,3,2,1,0:T(8,128)(2,1)S(1)}, u32[]{:S(2)}, u32[]{:S(2)}) %collective-permute-start.5) | collective-permute-done | bytes 983072 | tf_op jit(solution)/shard_map/ppermute | solution.py:18
  610.4 17.5 %collective-permute-done.6 = bf16[2,1,4,16,3840]{4,3,2,1,0:T(8,128)(2,1)S(1)} collective-permute-done((bf16[2,1,4,16,3840]{4,3,2,1,0:T(8,128)(2,1)S(1)}, bf16[2,1,4,16,3840]{4,3,2,1,0:T(8,128)(2,1)S(1)}, u32[]{:S(2)}, u32[]{:S(2)}) %collective-permute-start.6) | collective-permute-done | bytes 983072 | tf_op jit(solution)/shard_map/ppermute | solution.py:21
  627.9 2.6 pad_maximum_fusion.3
  630.6 1.7 collective-permute-start.8
  636.2 5.1 fusion.73
  641.3 3.7 copy.120
  644.9 2.0 copy.121
  646.9 17.0 %collective-permute-done.7 = bf16[2,1,24,4,3840]{4,3,2,1,0:T(4,128)(2,1)} collective-permute-done((bf16[2,1,24,4,3840]{4,3,2,1,0:T(4,128)(2,1)}, bf16[2,1,24,4,3840]{4,3,2,1,0:T(4,128)(2,1)}, u32[]{:S(2)}, u32[]{:S(2)}) %collective-permute-start.7) | collective-permute-done | bytes 1474592 | tf_op jit(solution)/shard_map/ppermute | solution.py:18
  664.2 8.7 %fusion.28 = bf16[2,1,16,16,3840]{4,3,2,1,0:T(8,128)(2,1)S(1)} fusion(s32[]{:T(128)S(6)} %select_n.31, s32[]{:T(128)S(6)} %select_n.32, bf16[2,1,24,4,3840]{4,3,2,1,0:T(4,128)(2,1)} %collective-permute-done.7, bf16[2,1,4,16,3840]{4,3,2,1,0:T(8,128)(2,1)} %copy-done.10, bf16[1,1,16,16,3840]{4,3,2,1,0:T(8,128)(2,1)S(1)} %bitcast.118, ...), kind=kLoop, calls=%fused_computation.39 | loop fusion | flops 23592960 | bytes 12779528 | tf_op jit(solution)/shard_map/concatenate | solution.py:22
  673.3 1.6 copy-done.7
  675.0 1.0 copy-done.12
  677.4 0.9 fusion.48
  679.4 1.1 fusion.50
  681.8 9.3 %collective-permute-start.10 = (bf16[2,1,5,16,1280]{4,3,2,1,0:T(8,128)(2,1)S(1)}, bf16[2,1,5,16,1280]{4,3,2,1,0:T(8,128)(2,1)S(1)}, u32[]{:S(2)}, u32[]{:S(2)}) collective-permute-start(bf16[2,1,5,16,1280]{4,3,2,1,0:T(8,128)(2,1)S(1)} %get-tuple-element.36), channel_id=1, source_target_pairs={{4,0},{8,4},{12,8},{0,12},{5,1},{9,5},{13,9},{1,13},{6,2},{10,6},{... | collective-permute-start | bytes 1228808 | tf_op jit(solution)/shard_map/ppermute | solution.py:21
  691.1 9.9 %collective-permute-done.10 = bf16[2,1,5,16,1280]{4,3,2,1,0:T(8,128)(2,1)S(1)} collective-permute-done((bf16[2,1,5,16,1280]{4,3,2,1,0:T(8,128)(2,1)S(1)}, bf16[2,1,5,16,1280]{4,3,2,1,0:T(8,128)(2,1)S(1)}, u32[]{:S(2)}, u32[]{:S(2)}) %collective-permute-start.10) | collective-permute-done | bytes 409632 | tf_op jit(solution)/shard_map/ppermute | solution.py:21
  701.0 8.5 %collective-permute-done.9 = bf16[2,1,5,16,1280]{4,3,2,1,0:T(8,128)(2,1)S(1)} collective-permute-done((bf16[2,1,5,16,1280]{4,3,2,1,0:T(8,128)(2,1)S(1)}, bf16[2,1,5,16,1280]{4,3,2,1,0:T(8,128)(2,1)S(1)}, u32[]{:S(2)}, u32[]{:S(2)}) %collective-permute-start.9) | collective-permute-done | bytes 409632 | tf_op jit(solution)/shard_map/ppermute | solution.py:18
  711.2 1.4 copy.109
  712.6 1.2 collective-permute-start.12
  716.7 8.8 %collective-permute-done.11 = bf16[2,1,26,5,1280]{4,0,3,2,1:T(2,128)(2,1)S(1)} collective-permute-done((bf16[2,1,26,5,1280]{4,0,3,2,1:T(2,128)(2,1)S(1)}, bf16[2,1,26,5,1280]{4,0,3,2,1:T(2,128)(2,1)S(1)}, u32[]{:S(2)}, u32[]{:S(2)}) %collective-permute-start.11) | collective-permute-done | bytes 665632 | tf_op jit(solution)/shard_map/ppermute | solution.py:18
  726.2 1.2 copy.111
  727.4 4.3 fusion.44
  731.7 4.0 fusion.52
  (74 shorter events, 10.4 us)
Async XLA Ops:
  6.5 557.8 %copy-start = (bf16[1,1,16,16,2560]{4,3,2,1,0:T(8,128)(2,1)S(1)}, bf16[1,1,16,16,2560]{4,3,2,1,0:T(8,128)(2,1)}, u32[]{:S(2)}) copy-start(bf16[1,1,16,16,2560]{4,3,2,1,0:T(8,128)(2,1)} %param.9) | copy-start | bytes 3932164
  6.5 42.1 %copy-start.8 = (bf16[80,3840]{1,0:T(8,128)(2,1)S(1)}, bf16[80,3840]{1,0:T(8,128)(2,1)}, u32[]{:S(2)}) copy-start(bf16[80,3840]{1,0:T(8,128)(2,1)} %param.11) | copy-start | bytes 1843204
  6.5 629.7 %all-gather.2.cloned.1.call-start = ((), (), s32[]{:S(2)}) async-start(), calls=%async_computation | async-start | bytes 1392640 | tf_op jit(solution)/shard_map/all_gather | solution.py:107
  6.5 14.4 %collective-permute-start = (bf16[80,3840]{1,0:T(8,128)(2,1)}, bf16[80,3840]{1,0:T(8,128)(2,1)S(1)}, u32[]{:S(2)}, u32[]{:S(2)}) collective-permute-start(bf16[80,3840]{1,0:T(8,128)(2,1)} %param.11), channel_id=1, source_target_pairs={{0,31},{1,0},{2,1},{3,2},{4,3},{5,4},{6,5},{7,6},{8,7},{9,8},{10,9... | collective-permute-start | bytes 1843208 | tf_op jit(solution)/shard_map/ppermute | solution.py:97
  20.9 87.4 %copy-start.9 = (bf16[80,3840]{1,0:T(8,128)(2,1)}, bf16[80,3840]{1,0:T(8,128)(2,1)S(1)}, u32[]{:S(2)}) copy-start(bf16[80,3840]{1,0:T(8,128)(2,1)S(1)} %collective-permute-done) | copy-start | bytes 1843204
  22.3 26.4 %collective-permute-start.1 = (bf16[160,3840]{1,0:T(8,128)(2,1)S(1)}, bf16[160,3840]{1,0:T(8,128)(2,1)S(1)}, u32[]{:S(2)}, u32[]{:S(2)}) collective-permute-start(bf16[160,3840]{1,0:T(8,128)(2,1)S(1)} %pad_maximum_fusion.7), channel_id=1, source_target_pairs={{0,30},{1,31},{2,0},{3,1},{4,2},{5,3},{6,4},{7,5},{8,6},{9,7},{10,... | collective-permute-start | bytes 3686408 | tf_op jit(solution)/shard_map/ppermute | solution.py:97
  48.8 55.4 %collective-permute-start.2 = (bf16[320,3840]{1,0:T(8,128)(2,1)S(1)}, bf16[320,3840]{1,0:T(8,128)(2,1)S(1)}, u32[]{:S(2)}, u32[]{:S(2)}) collective-permute-start(bf16[320,3840]{1,0:T(8,128)(2,1)S(1)} %pad_maximum_fusion.1), channel_id=1, source_target_pairs={{0,28},{1,29},{2,30},{3,31},{4,0},{5,1},{6,2},{7,3},{8,4},{9,5},{1... | collective-permute-start | bytes 7372808 | tf_op jit(solution)/shard_map/ppermute | solution.py:97
  104.3 6.2 copy-start.2
  104.7 214.9 %collective-permute-start.3 = (bf16[640,3840]{1,0:T(8,128)(2,1)S(1)}, bf16[640,3840]{1,0:T(8,128)(2,1)S(1)}, u32[]{:S(2)}, u32[]{:S(2)}) collective-permute-start(bf16[640,3840]{1,0:T(8,128)(2,1)S(1)} %pad_maximum_fusion), channel_id=1, source_target_pairs={{0,24},{1,25},{2,26},{3,27},{4,28},{5,29},{6,30},{7,31},{8,0},{9,1... | collective-permute-start | bytes 14745608 | tf_op jit(solution)/shard_map/ppermute | solution.py:97
  112.2 207.3 %copy-start.15 = (bf16[1280,3840]{1,0:T(8,128)(2,1)}, bf16[1280,3840]{1,0:T(8,128)(2,1)S(1)}, u32[]{:S(2)}) copy-start(bf16[1280,3840]{1,0:T(8,128)(2,1)S(1)} %get-tuple-element.28) | copy-start | bytes 29491204
  319.5 5.2 copy-start.4
  319.5 6.6 copy-start.14
  324.7 213.5 %collective-permute-start.4 = (bf16[1280,3840]{1,0:T(8,128)(2,1)}, bf16[1280,3840]{1,0:T(8,128)(2,1)}, u32[]{:S(2)}, u32[]{:S(2)}) collective-permute-start(bf16[1280,3840]{1,0:T(8,128)(2,1)} %get-tuple-element.24), channel_id=1, source_target_pairs={{0,16},{1,17},{2,18},{3,19},{4,20},{5,21},{6,22},{7,23},{8,24},{9,... | collective-permute-start | bytes 29491208 | tf_op jit(solution)/shard_map/ppermute | solution.py:97
  546.4 4.0 copy-start.3
  550.4 3.3 copy-start.5
  564.3 9.7 %copy-start.18 = (bf16[1,1,16,16,2560]{4,3,2,1,0:T(8,128)(2,1)S(1)}, bf16[1,1,16,16,2560]{4,3,2,1,0:T(8,128)(2,1)}, u32[]{:S(2)}) copy-start(bf16[1,1,16,16,2560]{4,3,2,1,0:T(8,128)(2,1)} %param.10) | copy-start | bytes 3932164
  583.7 44.2 %copy-start.6 = (bf16[3840,256]{0,1:T(8,128)(2,1)}, bf16[3840,256]{0,1:T(8,128)(2,1)S(1)}, u32[]{:S(2)}) copy-start(bf16[3840,256]{0,1:T(8,128)(2,1)S(1)} %fusion.21) | copy-start | bytes 5898244
  583.9 26.5 %collective-permute-start.5 = (bf16[2,1,4,16,3840]{4,3,2,1,0:T(8,128)(2,1)S(1)}, bf16[2,1,4,16,3840]{4,3,2,1,0:T(8,128)(2,1)S(1)}, u32[]{:S(2)}, u32[]{:S(2)}) collective-permute-start(bf16[2,1,4,16,3840]{4,3,2,1,0:T(8,128)(2,1)S(1)} %get-tuple-element.26), channel_id=1, source_target_pairs={{0,4},{4,8},{8,12},{12,0},{1,5},{5,9},{9,13},{13,1},{2,6},{6,10},{... | collective-permute-start | bytes 2949128 | tf_op jit(solution)/shard_map/ppermute | solution.py:18
  584.0 48.3 %copy-start.17 = (s32[1,2]{1,0:T(1,128)S(1)}, s32[1,2]{1,0:T(1,128)}, u32[]{:S(2)}) copy-start(s32[1,2]{1,0:T(1,128)} %param.14) | copy-start | bytes 28
  584.0 43.9 %collective-permute-start.6 = (bf16[2,1,4,16,3840]{4,3,2,1,0:T(8,128)(2,1)S(1)}, bf16[2,1,4,16,3840]{4,3,2,1,0:T(8,128)(2,1)S(1)}, u32[]{:S(2)}, u32[]{:S(2)}) collective-permute-start(bf16[2,1,4,16,3840]{4,3,2,1,0:T(8,128)(2,1)S(1)} %get-tuple-element.27), channel_id=1, source_target_pairs={{4,0},{8,4},{12,8},{0,12},{5,1},{9,5},{13,9},{1,13},{6,2},{10,6},{... | collective-permute-start | bytes 2949128 | tf_op jit(solution)/shard_map/ppermute | solution.py:21
  610.4 20.1 %copy-start.10 = (bf16[2,1,4,16,3840]{4,3,2,1,0:T(8,128)(2,1)}, bf16[2,1,4,16,3840]{4,3,2,1,0:T(8,128)(2,1)S(1)}, u32[]{:S(2)}) copy-start(bf16[2,1,4,16,3840]{4,3,2,1,0:T(8,128)(2,1)S(1)} %collective-permute-done.5) | copy-start | bytes 2949124
  627.9 2.6 copy-start.11
  630.5 33.5 %collective-permute-start.7 = (bf16[2,1,24,4,3840]{4,3,2,1,0:T(4,128)(2,1)}, bf16[2,1,24,4,3840]{4,3,2,1,0:T(4,128)(2,1)}, u32[]{:S(2)}, u32[]{:S(2)}) collective-permute-start(bf16[2,1,24,4,3840]{4,3,2,1,0:T(4,128)(2,1)} %get-tuple-element.23), channel_id=1, source_target_pairs={{0,1},{1,2},{2,3},{3,0},{4,5},{5,6},{6,7},{7,4},{8,9},{9,10},{10,1... | collective-permute-start | bytes 4423688 | tf_op jit(solution)/shard_map/ppermute | solution.py:18
  630.6 33.6 %collective-permute-start.8 = (bf16[2,1,24,4,3840]{4,3,2,1,0:T(4,128)(2,1)}, bf16[2,1,24,4,3840]{4,3,2,1,0:T(4,128)(2,1)}, u32[]{:S(2)}, u32[]{:S(2)}) collective-permute-start(bf16[2,1,24,4,3840]{4,3,2,1,0:T(4,128)(2,1)} %get-tuple-element.22), channel_id=1, source_target_pairs={{1,0},{2,1},{3,2},{0,3},{5,4},{6,5},{7,6},{4,7},{9,8},{10,9},{11,1... | collective-permute-start | bytes 4423688 | tf_op jit(solution)/shard_map/ppermute | solution.py:21
  673.0 1.9 copy-start.7
  674.8 1.1 copy-start.12
  678.3 1.1 copy-start.13
  681.8 19.2 %collective-permute-start.10 = (bf16[2,1,5,16,1280]{4,3,2,1,0:T(8,128)(2,1)S(1)}, bf16[2,1,5,16,1280]{4,3,2,1,0:T(8,128)(2,1)S(1)}, u32[]{:S(2)}, u32[]{:S(2)}) collective-permute-start(bf16[2,1,5,16,1280]{4,3,2,1,0:T(8,128)(2,1)S(1)} %get-tuple-element.36), channel_id=1, source_target_pairs={{4,0},{8,4},{12,8},{0,12},{5,1},{9,5},{13,9},{1,13},{6,2},{10,6},{... | collective-permute-start | bytes 1228808 | tf_op jit(solution)/shard_map/ppermute | solution.py:21
  691.1 18.4 %collective-permute-start.9 = (bf16[2,1,5,16,1280]{4,3,2,1,0:T(8,128)(2,1)S(1)}, bf16[2,1,5,16,1280]{4,3,2,1,0:T(8,128)(2,1)S(1)}, u32[]{:S(2)}, u32[]{:S(2)}) collective-permute-start(bf16[2,1,5,16,1280]{4,3,2,1,0:T(8,128)(2,1)S(1)} %get-tuple-element.35), channel_id=1, source_target_pairs={{0,4},{4,8},{8,12},{12,0},{1,5},{5,9},{9,13},{13,1},{2,6},{6,10},{... | collective-permute-start | bytes 1228808 | tf_op jit(solution)/shard_map/ppermute | solution.py:18
  710.1 6.4 copy-start.16
  710.7 14.8 %collective-permute-start.11 = (bf16[2,1,26,5,1280]{4,0,3,2,1:T(2,128)(2,1)S(1)}, bf16[2,1,26,5,1280]{4,0,3,2,1:T(2,128)(2,1)S(1)}, u32[]{:S(2)}, u32[]{:S(2)}) collective-permute-start(bf16[2,1,26,5,1280]{4,0,3,2,1:T(2,128)(2,1)S(1)} %copy.108), channel_id=1, source_target_pairs={{0,1},{1,2},{2,3},{3,0},{4,5},{5,6},{6,7},{7,4},{8,9},{9,10},{10,1... | collective-permute-start | bytes 1996808 | tf_op jit(solution)/shard_map/ppermute | solution.py:18
  712.6 13.6 %collective-permute-start.12 = (bf16[2,1,26,5,1280]{4,0,3,2,1:T(2,128)(2,1)}, bf16[2,1,26,5,1280]{4,0,3,2,1:T(2,128)(2,1)}, u32[]{:S(2)}, u32[]{:S(2)}) collective-permute-start(bf16[2,1,26,5,1280]{4,0,3,2,1:T(2,128)(2,1)} %copy.109), channel_id=1, source_target_pairs={{1,0},{2,1},{3,2},{0,3},{5,4},{6,5},{7,6},{4,7},{9,8},{10,9},{11,1... | collective-permute-start | bytes 1996808 | tf_op jit(solution)/shard_map/ppermute | solution.py:21
  731.7 4.1 copy-start.1
Sparse Core Ops, SparseCore 0:
  327.0 36.7 all-gather.1
